TPU v7x, 32 devices: a whole 2x2x4 slice. The times are simulated.
32 devices in a mesh: dp: 4 (over z), ulysses: 8 (over y, x, core).
Axes of the slice: x: 2, y: 2, z: 4, core: 2. Of those that a mesh axis runs over, the one named last changes fastest.
Arguments:
- q_raw: bfloat16 [4, 1024, 3072], P('dp', 'ulysses')
- k_raw: bfloat16 [4, 1024, 3072], P('dp', 'ulysses')
- values: bfloat16 [4, 1024, 3072], P('dp', 'ulysses'), may hold values from -6 to 6
- grad_out: bfloat16 [4, 1024, 3072], P('dp', 'ulysses'), may hold values from -6 to 6
- q_gain: float32 [128], replicated
- k_gain: float32 [128], replicated
- block_masks: int32 [24, 8, 8], replicated, may hold values from 0 to 1, as said below
Outputs:
- grad_q_raw: bfloat16 [4, 1024, 3072], P('dp', 'ulysses')
- grad_k_raw: bfloat16 [4, 1024, 3072], P('dp', 'ulysses')
- grad_values: bfloat16 [4, 1024, 3072], P('dp', 'ulysses')
- gain_grads: float32 [2, 128], replicated
Inputs may be any that keep to these rules, and one draw needn't show every extreme that they name: `block_masks`: every diagonal block is 1. A third of the heads are dense with some blocks missing, a third keep a band of neighbouring blocks, a third keep blocks a fixed stride apart; which heads are which is drawn.
All inputs are finite; a program needn't handle non-finite values.
Results may differ from a plain program's by a relative error of at most 0.0045.
The roundings to bfloat16 on the way count: a program that leaves them out, or rounds other values in their place, can miss the bound.
Values may be sent and summed in bfloat16 or wider, within the bound.
A program may use at most 64 MiB of HBM per device.

v0:
```python
import functools
import math

import jax
import jax.numpy as jnp
from jax import lax
from jax.experimental import pallas as pl
from jax.experimental.pallas import tpu as pltpu
from jax.sharding import PartitionSpec as P

HEADS = 24
HEAD_DIM = 128
SPLITS = 8
BLOCK = 128
TILE = 512
ITEMS = 32


norm_eps = 1e-06
neg_fill = -1e30


def rms_norm(raw, gain):
    raw_float = raw.astype(jnp.float32)
    spread = jnp.sqrt(jnp.mean(raw_float * raw_float, axis=-1, keepdims=True) + norm_eps)
    return (raw_float, spread, (raw_float / spread * gain).astype(jnp.bfloat16))


def norm_back(raw_float, spread, gain, grad_normed):
    inner = jnp.sum(gain * grad_normed * raw_float, axis=-1, keepdims=True)
    return gain * grad_normed / spread - raw_float * inner / (HEAD_DIM * spread**3)


def dot_rows(left_side, right_side):
    return lax.dot_general(
        left_side, right_side, (((1,), (1,)), ((), ())), preferred_element_type=jnp.float32
    )


def dot_cols(left_side, right_side):
    return lax.dot_general(
        left_side, right_side, (((0,), (0,)), ((), ())), preferred_element_type=jnp.float32
    )


def rows_of(source, tile_index):
    return lax.dynamic_slice_in_dim(source, tile_index * TILE, TILE, 0)


def add_rows(target, addend, tile_index):
    return lax.dynamic_update_slice_in_dim(
        target, rows_of(target, tile_index) + addend, tile_index * TILE, 0
    )


def plan_items(block_masks, unit_count):
    block_count = block_masks.shape[1]
    per_unit = ITEMS // unit_count
    head_ids = jnp.arange(HEADS, dtype=jnp.int32)
    weight = jnp.sum(block_masks, axis=(1, 2))
    order = jnp.argsort(-(weight * HEADS + head_ids))
    heavy_heads = order[:SPLITS]
    light_heads = order[SPLITS:]
    counter = jnp.arange(2 * SPLITS, dtype=jnp.int32)
    item_head = jnp.concatenate([heavy_heads[counter // 2], light_heads])
    item_half = jnp.concatenate([1 + counter % 2, jnp.zeros((HEADS - SPLITS,), jnp.int32)])
    upper = jnp.sum(block_masks[:, : block_count // 2, :], axis=(1, 2))
    lower = weight - upper
    item_weight = jnp.where(
        item_half == 0,
        weight[item_head],
        jnp.where(item_half == 1, upper[item_head], lower[item_head]),
    )
    ranked = jnp.argsort(-(item_weight * ITEMS + jnp.arange(ITEMS, dtype=jnp.int32)))
    places = jnp.arange(ITEMS, dtype=jnp.int32)
    rounds = places // unit_count
    column = places % unit_count
    device = jnp.where(rounds % 2 == 0, column, unit_count - 1 - column)
    target = device * per_unit + rounds
    plan_head = jnp.zeros((ITEMS,), jnp.int32).at[target].set(item_head[ranked])
    plan_half = jnp.zeros((ITEMS,), jnp.int32).at[target].set(item_half[ranked])
    return (plan_head, plan_half)


def item_grads(columns, mask_head, half_code, q_gain, k_gain):
    seq_len = columns.shape[0]
    q_float, q_spread, q_normed = rms_norm(columns[:, :HEAD_DIM], q_gain)
    k_float, k_spread, k_normed = rms_norm(columns[:, HEAD_DIM : 2 * HEAD_DIM], k_gain)
    v_rows = columns[:, 2 * HEAD_DIM : 3 * HEAD_DIM]
    o_grads = columns[:, 3 * HEAD_DIM :]
    tile_count = seq_len // TILE
    tile_blocks = TILE // BLOCK
    active = (
        jnp.max(mask_head.reshape(tile_count, tile_blocks, tile_count, tile_blocks), axis=(1, 3))
        > 0
    )
    first_tile = jnp.where(half_code == 2, tile_count // 2, 0)
    last_tile = jnp.where(half_code == 1, tile_count // 2, tile_count)
    score_scale = HEAD_DIM ** (-0.5)

    def allowed_at(row_tile, col_tile):
        blocks = lax.dynamic_slice(
            mask_head, (row_tile * tile_blocks, col_tile * tile_blocks), (tile_blocks, tile_blocks)
        )
        return jnp.repeat(jnp.repeat(blocks, BLOCK, 0), BLOCK, 1) > 0

    def query_tile(row_tile, carry):
        grad_qn, grad_kn, grad_v = carry
        q_tile = rows_of(q_normed, row_tile)
        o_tile = rows_of(o_grads, row_tile)

        def stats_step(col_tile, stats):

            def stats_visit(stats_in):
                run_max, run_sum, run_dot = stats_in
                allowed = allowed_at(row_tile, col_tile)
                scores = jnp.where(
                    allowed, dot_rows(q_tile, rows_of(k_normed, col_tile)) * score_scale, neg_fill
                )
                grad_weights = dot_rows(o_tile, rows_of(v_rows, col_tile))
                new_max = jnp.maximum(run_max, jnp.max(scores, axis=1, keepdims=True))
                weights = jnp.where(allowed, jnp.exp(scores - new_max), 0.0)
                rescale = jnp.exp(run_max - new_max)
                return (
                    new_max,
                    run_sum * rescale + jnp.sum(weights, axis=1, keepdims=True),
                    run_dot * rescale + jnp.sum(weights * grad_weights, axis=1, keepdims=True),
                )

            return lax.cond(
                active[row_tile, col_tile], stats_visit, lambda unchanged: unchanged, stats
            )

        start = (
            jnp.full((TILE, 1), neg_fill, jnp.float32),
            jnp.zeros((TILE, 1), jnp.float32),
            jnp.zeros((TILE, 1), jnp.float32),
        )
        run_max, run_sum, run_dot = lax.fori_loop(0, tile_count, stats_step, start)
        log_total = run_max + jnp.log(run_sum)
        row_delta = run_dot / run_sum

        def grad_step(col_tile, inner):

            def grad_visit(inner_in):
                tile_dq, grad_keys, grad_vals = inner_in
                allowed = allowed_at(row_tile, col_tile)
                k_tile = rows_of(k_normed, col_tile)
                v_tile = rows_of(v_rows, col_tile)
                scores = jnp.where(allowed, dot_rows(q_tile, k_tile) * score_scale, neg_fill)
                weights = jnp.where(allowed, jnp.exp(scores - log_total), 0.0)
                grad_weights = dot_rows(o_tile, v_tile)
                grad_scores = weights * (grad_weights - row_delta)
                weights_half = weights.astype(jnp.bfloat16)
                scores_half = grad_scores.astype(jnp.bfloat16)
                tile_dq = (
                    tile_dq
                    + jnp.dot(scores_half, k_tile, preferred_element_type=jnp.float32) * score_scale
                )
                grad_keys = add_rows(
                    grad_keys, dot_cols(scores_half, q_tile) * score_scale, col_tile
                )
                grad_vals = add_rows(grad_vals, dot_cols(weights_half, o_tile), col_tile)
                return (tile_dq, grad_keys, grad_vals)

            return lax.cond(
                active[row_tile, col_tile], grad_visit, lambda unchanged: unchanged, inner
            )

        tile_dq, grad_kn, grad_v = lax.fori_loop(
            0, tile_count, grad_step, (jnp.zeros((TILE, HEAD_DIM), jnp.float32), grad_kn, grad_v)
        )
        grad_qn = lax.dynamic_update_slice_in_dim(grad_qn, tile_dq, row_tile * TILE, 0)
        return (grad_qn, grad_kn, grad_v)

    empty = jnp.zeros((seq_len, HEAD_DIM), jnp.float32)
    grad_qn, grad_kn, grad_v = lax.fori_loop(
        first_tile, last_tile, query_tile, (empty, empty, empty)
    )
    grad_q = norm_back(q_float, q_spread, q_gain, grad_qn)
    grad_k = norm_back(k_float, k_spread, k_gain, grad_kn)
    gain_part = jnp.stack(
        [
            jnp.sum(grad_qn * q_float / q_spread, axis=0),
            jnp.sum(grad_kn * k_float / k_spread, axis=0),
        ]
    )
    return (jnp.concatenate([grad_q, grad_k, grad_v], axis=1), gain_part)


def body(q_raw, k_raw, values, grad_out, q_gain, k_gain, block_masks):
    unit_count = lax.axis_size("ulysses")
    group_count = lax.axis_size("dp")
    device_rank = lax.axis_index("ulysses")
    videos_here, tok_rows, width = q_raw.shape
    seq_len = tok_rows * unit_count
    per_unit = ITEMS // unit_count
    item_heads, item_halves = plan_items(block_masks, unit_count)
    stacked = jnp.concatenate(
        [
            operand.reshape(videos_here, tok_rows, HEADS, HEAD_DIM)
            for operand in (q_raw, k_raw, values, grad_out)
        ],
        axis=3,
    )
    picked = jnp.take(stacked, item_heads, axis=2)
    outgoing = picked.transpose(2, 0, 1, 3).reshape(
        unit_count, per_unit, videos_here, tok_rows, 4 * HEAD_DIM
    )
    arrived = lax.all_to_all(outgoing, "ulysses", split_axis=0, concat_axis=3, tiled=True)
    results = []
    gain_total = jnp.zeros((2, HEAD_DIM), jnp.float32)
    for item_slot in range(per_unit):
        item_index = device_rank * per_unit + item_slot
        head_index = item_heads[item_index]
        half_code = item_halves[item_index]
        mask_head = lax.dynamic_index_in_dim(block_masks, head_index, 0, keepdims=False)
        item_grad, gain_part = item_grads(
            arrived[0, item_slot, 0], mask_head, half_code, q_gain, k_gain
        )
        video_rows = [item_grad]
        gain_total = gain_total + gain_part
        results.append(jnp.stack(video_rows))
    backward = jnp.stack(results)[None]
    returned = lax.all_to_all(
        backward.astype(jnp.bfloat16), "ulysses", split_axis=3, concat_axis=0, tiled=True
    ).astype(backward.dtype)
    returned = returned.reshape(ITEMS, videos_here, tok_rows, 3 * HEAD_DIM)
    selector = (item_heads[:, None] == jnp.arange(HEADS)[None, :]).astype(jnp.float32)
    merged = jnp.einsum("ih,ivtc->vthc", selector, returned, precision=lax.Precision.HIGHEST)
    grad_q_raw = merged[..., :HEAD_DIM].reshape(videos_here, tok_rows, width).astype(jnp.bfloat16)
    grad_k_raw = (
        merged[..., HEAD_DIM : 2 * HEAD_DIM]
        .reshape(videos_here, tok_rows, width)
        .astype(jnp.bfloat16)
    )
    grad_values = (
        merged[..., 2 * HEAD_DIM :].reshape(videos_here, tok_rows, width).astype(jnp.bfloat16)
    )
    summed = lax.psum(gain_total, ("dp", "ulysses"))
    gain_grads = summed * (group_count * videos_here * seq_len * HEADS) ** (-0.5)
    return (grad_q_raw, grad_k_raw, grad_values, gain_grads)


QUERY_TILE = 256
KERNEL_BYTES = 24 * 2**20
MESH = pl.DeviceIdType.MESH


def aligned(index, size):
    return pl.ds(pl.multiple_of(index * size, size), size)


def head_work(slot, arrived, results, gain_acc, gains, scratch):
    bias, q_norm, k_norm, k_cols, grad_qn, grad_kn, grad_v, scores, grads, probs_half, grads_half = scratch
    seq_len = arrived.shape[2]
    block_count = seq_len // BLOCK
    score_scale = HEAD_DIM ** (-0.5)
    exponent_scale = score_scale * math.log2(math.e)

    def normed(which):
        raw = arrived[slot, which].astype(jnp.float32)
        inverse = 1.0 / jnp.sqrt(jnp.mean(raw * raw, axis=1, keepdims=True) + norm_eps)
        return raw * inverse * gains[which][...]

    q_norm[...] = normed(0).astype(jnp.bfloat16)
    k_float = normed(1)
    k_norm[...] = k_float.astype(jnp.bfloat16)
    k_cols[...] = k_float.T.astype(jnp.bfloat16)
    grad_kn[...] = jnp.zeros_like(grad_kn)
    grad_v[...] = jnp.zeros_like(grad_v)

    def tile_step(tile, carry):
        rows = aligned(tile, QUERY_TILE)
        q_tile = q_norm[rows, :]
        o_tile = arrived[slot, 3, rows, :]
        shifts = bias[:, rows]
        peak = jnp.full((1, QUERY_TILE), -jnp.inf, jnp.float32)
        for block in range(block_count):
            keys = pl.ds(block * BLOCK, BLOCK)
            block_scores = dot_rows(k_norm[keys, :], q_tile)
            scores[keys, :] = block_scores
            block_peak = jnp.max(block_scores, axis=0, keepdims=True) * exponent_scale
            peak = jnp.maximum(peak, block_peak + shifts[block : block + 1, :])
        total = jnp.zeros((1, QUERY_TILE), jnp.float32)
        row_dot = jnp.zeros((1, QUERY_TILE), jnp.float32)
        for block in range(block_count):
            keys = pl.ds(block * BLOCK, BLOCK)
            offset = shifts[block : block + 1, :] - peak
            weights = jnp.exp2(scores[keys, :] * exponent_scale + offset)
            grad_weights = dot_rows(arrived[slot, 2, keys, :], o_tile)
            scores[keys, :] = weights
            grads[keys, :] = grad_weights
            total = total + jnp.sum(weights, axis=0, keepdims=True)
            row_dot = row_dot + jnp.sum(weights * grad_weights, axis=0, keepdims=True)
        inverse = 1.0 / total
        delta = row_dot * inverse
        for block in range(block_count):
            keys = pl.ds(block * BLOCK, BLOCK)
            weights = scores[keys, :] * inverse
            probs_half[keys, :] = weights.astype(jnp.bfloat16)
            grads_half[keys, :] = (weights * (grads[keys, :] - delta)).astype(jnp.bfloat16)
        grad_v[...] += jnp.dot(probs_half[...], o_tile, preferred_element_type=jnp.float32)
        grad_kn[...] += jnp.dot(grads_half[...], q_tile, preferred_element_type=jnp.float32)
        turned = jnp.dot(k_cols[...], grads_half[...], preferred_element_type=jnp.float32)
        grad_qn[rows, :] = turned.T
        return carry

    lax.fori_loop(0, seq_len // QUERY_TILE, tile_step, 0)
    results[slot, 2] = grad_v[...].astype(jnp.bfloat16)
    for which, grad_normed in ((0, grad_qn), (1, grad_kn)):
        raw = arrived[slot, which].astype(jnp.float32)
        inverse = 1.0 / jnp.sqrt(jnp.mean(raw * raw, axis=1, keepdims=True) + norm_eps)
        unit = raw * inverse
        grad = grad_normed[...] * score_scale
        gain_acc[which : which + 1, :] += jnp.sum(grad * unit, axis=0, keepdims=True)
        scaled = grad * gains[which][...]
        inner = jnp.mean(scaled * unit, axis=1, keepdims=True)
        results[slot, which] = ((scaled - unit * inner) * inverse).astype(jnp.bfloat16)


def exchange_kernel(
    units, groups, gain_scale,
    q_raw, k_raw, values, grad_out, q_gain_in, k_gain_in, masks_in,
    out_q, out_k, out_v, out_gain,
    arrived, results, gain_units, gain_groups, gain_acc,
    in_send, in_recv, in_own, out_send, out_recv, out_own,
    unit_send, unit_recv, group_send, group_recv, small_sem, q_gain, k_gain, masks, *scratch,
):
    me = lax.axis_index("ulysses")
    group = lax.axis_index("dp")
    slots, _, seq_len, _ = arrived.shape
    tok_rows = seq_len // units
    sources = (q_raw, k_raw, values, grad_out)
    targets = (out_q, out_k, out_v)

    bits = units.bit_length() - 1
    paired = units == 2**bits

    def unit_at(offset):
        if not paired:
            return lax.rem(me + offset % units, units)
        places = (lax.rem(me // 2**bit + offset // 2**bit, 2) * 2**bit for bit in range(bits))
        return sum(places, jnp.int32(0))

    def sender_at(offset):
        return unit_at(offset if paired else units - offset)

    offsets = sorted(range(1, units), key=lambda offset: (-(offset // 2).bit_count(), offset % 2, offset))

    def group_at(offset):
        return lax.rem(group + offset, groups)

    def inward(slot, which, offset):
        owner = unit_at(offset)
        return pltpu.make_async_remote_copy(
            src_ref=sources[which].at[0, :, aligned(owner * slots + slot, HEAD_DIM)],
            dst_ref=arrived.at[slot, which, aligned(me, tok_rows), :],
            send_sem=in_send.at[slot, which, offset],
            recv_sem=in_recv.at[slot, which, offset],
            device_id={"ulysses": owner},
            device_id_type=MESH,
        )

    def inward_own(slot, which):
        return pltpu.make_async_copy(
            sources[which].at[0, :, aligned(me * slots + slot, HEAD_DIM)],
            arrived.at[slot, which, aligned(me, tok_rows), :],
            in_own.at[slot, which],
        )

    def inward_from(slot, which, offset):
        owner = sender_at(offset)
        landed = arrived.at[slot, which, aligned(owner, tok_rows), :]
        return pltpu.make_async_remote_copy(
            src_ref=landed,
            dst_ref=landed,
            send_sem=in_send.at[slot, which, offset],
            recv_sem=in_recv.at[slot, which, offset],
            device_id={"ulysses": owner},
            device_id_type=MESH,
        )

    def outward(slot, which, offset):
        owner = unit_at(offset)
        return pltpu.make_async_remote_copy(
            src_ref=results.at[slot, which, aligned(owner, tok_rows), :],
            dst_ref=targets[which].at[0, :, aligned(me * slots + slot, HEAD_DIM)],
            send_sem=out_send.at[slot, which, offset],
            recv_sem=out_recv.at[slot, which, offset],
            device_id={"ulysses": owner},
            device_id_type=MESH,
        )

    def outward_own(slot, which):
        return pltpu.make_async_copy(
            results.at[slot, which, aligned(me, tok_rows), :],
            targets[which].at[0, :, aligned(me * slots + slot, HEAD_DIM)],
            out_own.at[slot, which],
        )

    def outward_from(slot, which, offset):
        owner = sender_at(offset)
        landed = targets[which].at[0, :, aligned(owner * slots + slot, HEAD_DIM)]
        return pltpu.make_async_remote_copy(
            src_ref=landed,
            dst_ref=landed,
            send_sem=out_send.at[slot, which, offset],
            recv_sem=out_recv.at[slot, which, offset],
            device_id={"ulysses": owner},
            device_id_type=MESH,
        )

    def gain_to(buffer, place, axis, target, send_sem, recv_sem):
        return pltpu.make_async_remote_copy(
            src_ref=buffer.at[place],
            dst_ref=buffer.at[place],
            send_sem=send_sem,
            recv_sem=recv_sem,
            device_id={axis: target},
            device_id_type=MESH,
        )

    small_copies = [
        pltpu.make_async_copy(source, target, small_sem.at[place])
        for place, (source, target) in enumerate(
            ((q_gain_in, q_gain), (k_gain_in, k_gain), (masks_in, masks))
        )
    ]
    barrier = pltpu.get_barrier_semaphore()
    for offset in offsets:
        pl.semaphore_signal(barrier, inc=1, device_id={"ulysses": unit_at(offset)}, device_id_type=MESH)
    for offset in range(1, groups):
        pl.semaphore_signal(barrier, inc=1, device_id={"dp": group_at(offset)}, device_id_type=MESH)
    for copy in small_copies:
        copy.start()
    for slot in range(slots):
        for which in range(4):
            inward_own(slot, which).start()
    pl.semaphore_wait(barrier, units + groups - 2)

    def send_slot(slot, carry):
        for offset in offsets:
            for which in range(4):
                inward(slot, which, offset).start()
        return carry

    lax.fori_loop(0, slots, send_slot, 0)
    gain_acc[...] = jnp.zeros_like(gain_acc)
    for copy in small_copies:
        copy.wait()
    bias = scratch[0]
    block_count = masks.shape[0]

    def work_slot(slot, carry):
        columns = lax.broadcasted_iota(jnp.int32, (block_count, HEADS), 1)
        for block in range(block_count):
            allowed = jnp.where(columns == me * slots + slot, masks[block].astype(jnp.float32), 0.0)
            allowed = jnp.sum(allowed, axis=1, keepdims=True)
            shift = jnp.where(allowed > 0.0, 0.0, -jnp.inf)
            bias[:, block * BLOCK : (block + 1) * BLOCK] = jnp.broadcast_to(shift, (block_count, BLOCK))
        for which in range(4):
            inward_own(slot, which).wait()
            for offset in offsets:
                inward_from(slot, which, offset).wait_recv()
        head_work(slot, arrived, results, gain_acc, (q_gain, k_gain), scratch)

        @pl.when(slot == slots - 1)
        def _():
            gain_units[me] = gain_acc[...]
            for offset in offsets:
                gain_to(
                    gain_units, me, "ulysses", unit_at(offset), unit_send.at[offset], unit_recv.at[offset]
                ).start()

        for offset in offsets:
            for which in range(3):
                outward(slot, which, offset).start()
        for which in range(3):
            outward_own(slot, which).start()
        return carry

    lax.fori_loop(0, slots, work_slot, 0)

    for offset in offsets:
        sender = sender_at(offset)
        gain_to(
            gain_units, sender, "ulysses", sender, unit_send.at[offset], unit_recv.at[offset]
        ).wait_recv()
    gain_groups[group] = jnp.sum(gain_units[...], axis=0)
    for offset in range(1, groups):
        gain_to(
            gain_groups, group, "dp", group_at(offset), group_send.at[offset], group_recv.at[offset]
        ).start()
    for offset in range(1, groups):
        sender = group_at(groups - offset)
        gain_to(
            gain_groups, sender, "dp", sender, group_send.at[offset], group_recv.at[offset]
        ).wait_recv()
    out_gain[...] = jnp.sum(gain_groups[...], axis=0)[:2] * gain_scale

    def drain_slot(slot, carry):
        for offset in offsets:
            for which in range(4):
                inward(slot, which, offset).wait_send()
            for which in range(3):
                outward(slot, which, offset).wait_send()
                outward_from(slot, which, offset).wait_recv()
        for which in range(3):
            outward_own(slot, which).wait()
        return carry

    lax.fori_loop(0, slots, drain_slot, 0)
    for offset in offsets:
        gain_to(
            gain_units, me, "ulysses", unit_at(offset), unit_send.at[offset], unit_recv.at[offset]
        ).wait_send()
    for offset in range(1, groups):
        gain_to(
            gain_groups, group, "dp", group_at(offset), group_send.at[offset], group_recv.at[offset]
        ).wait_send()


def hand_on_kernel(*refs):
    *arrays, sems = refs
    copies = [
        pltpu.make_async_copy(arrays[place], arrays[place + 4], sems.at[place]) for place in range(4)
    ]
    for copy in copies:
        copy.start()
    for copy in copies:
        copy.wait()


def exchange_body(q_raw, k_raw, values, grad_out, q_gain, k_gain, block_masks):
    units = lax.axis_size("ulysses")
    groups = lax.axis_size("dp")
    _, tok_rows, width = q_raw.shape
    seq_len = tok_rows * units
    slots = HEADS // units
    block_count = block_masks.shape[1]
    gain_scale = (groups * seq_len * HEADS) ** (-0.5)
    in_vmem = pl.BlockSpec(memory_space=pltpu.VMEM)
    in_hbm = pl.BlockSpec(memory_space=pltpu.HBM)
    anywhere = pl.BlockSpec(memory_space=pl.ANY)
    shard = jax.ShapeDtypeStruct((1, tok_rows, width), jnp.bfloat16)
    half = jnp.bfloat16
    full = jnp.float32
    dma = pltpu.SemaphoreType.DMA
    operands = (
        q_raw, k_raw, values, grad_out,
        q_gain.reshape(1, HEAD_DIM), k_gain.reshape(1, HEAD_DIM), block_masks.transpose(1, 2, 0),
    )
    grad_q, grad_k, grad_v, gain_grads = pl.pallas_call(
        functools.partial(exchange_kernel, units, groups, gain_scale),
        out_shape=(shard, shard, shard, jax.ShapeDtypeStruct((2, HEAD_DIM), full)),
        in_specs=[in_hbm] * 7,
        out_specs=(anywhere, anywhere, anywhere, in_vmem),
        scratch_shapes=[
            pltpu.VMEM((slots, 4, seq_len, HEAD_DIM), half),
            pltpu.VMEM((slots, 3, seq_len, HEAD_DIM), half),
            pltpu.VMEM((units, 8, HEAD_DIM), full),
            pltpu.VMEM((groups, 8, HEAD_DIM), full),
            pltpu.VMEM((8, HEAD_DIM), full),
            dma((slots, 4, units)),
            dma((slots, 4, units)),
            dma((slots, 4)),
            dma((slots, 3, units)),
            dma((slots, 3, units)),
            dma((slots, 3)),
            dma((units,)),
            dma((units,)),
            dma((groups,)),
            dma((groups,)),
            dma((3,)),
            pltpu.VMEM((1, HEAD_DIM), full),
            pltpu.VMEM((1, HEAD_DIM), full),
            pltpu.VMEM((block_count, block_count, HEADS), jnp.int32),
            pltpu.VMEM((block_count, seq_len), full),
            pltpu.VMEM((seq_len, HEAD_DIM), half),
            pltpu.VMEM((seq_len, HEAD_DIM), half),
            pltpu.VMEM((HEAD_DIM, seq_len), half),
            pltpu.VMEM((seq_len, HEAD_DIM), full),
            pltpu.VMEM((seq_len, HEAD_DIM), full),
            pltpu.VMEM((seq_len, HEAD_DIM), full),
            pltpu.VMEM((seq_len, QUERY_TILE), full),
            pltpu.VMEM((seq_len, QUERY_TILE), full),
            pltpu.VMEM((seq_len, QUERY_TILE), half),
            pltpu.VMEM((seq_len, QUERY_TILE), half),
        ],
        compiler_params=pltpu.CompilerParams(collective_id=0, has_side_effects=True, vmem_limit_bytes=KERNEL_BYTES),
    )(
        *(pltpu.with_memory_space_constraint(operand, pltpu.HBM) for operand in operands)
    )
    small = jax.ShapeDtypeStruct((2, HEAD_DIM), full)
    return pl.pallas_call(
        hand_on_kernel,
        out_shape=(shard, shard, shard, small),
        in_specs=[anywhere] * 4,
        out_specs=[in_hbm] * 4,
        scratch_shapes=[dma((4,))],
        compiler_params=pltpu.CompilerParams(vmem_limit_bytes=2**20),
    )(grad_q, grad_k, grad_v, gain_grads)


def solution(mesh):
    units = mesh.shape["ulysses"]

    def chosen(q_raw, *rest):
        if HEADS % units == 0 and q_raw.shape[0] == 1:
            return exchange_body(q_raw, *rest)
        return body(q_raw, *rest)

    return jax.shard_map(
        chosen,
        mesh=mesh,
        in_specs=(
            P("dp", "ulysses", None),
            P("dp", "ulysses", None),
            P("dp", "ulysses", None),
            P("dp", "ulysses", None),
            P(),
            P(),
            P(),
        ),
        out_specs=(
            P("dp", "ulysses", None),
            P("dp", "ulysses", None),
            P("dp", "ulysses", None),
            P(),
        ),
        check_vma=False,
    )
```

profile of v0, /device:TPU:1, one launch (start us, length us, event | category | flops | bytes accessed | tf_op | source)
XLA Modules:
  0.0 71.7 jit_solution(8113261515799850057)
XLA Ops:
  0.6 69.6 %shard_map.102 = (bf16[1,128,3072]{2,1,0:T(8,128)(2,1)S(1)}, bf16[1,128,3072]{2,1,0:T(8,128)(2,1)S(1)}, bf16[1,128,3072]{2,1,0:T(8,128)(2,1)S(1)}, f32[2,128]{1,0:T(2,128)S(1)}) custom-call(bf16[1,128,3072]{2,1,0:T(8,128)(2,1)} %q_raw.1, bf16[1,128,3072]{2,1,0:T(8,128)(2,1)} %k_raw.1, bf16[1,128,3072]{2,1,0:T(8,128)(2,1)} %values.1, ...), custom_call_target="tpu_custom_call" | custom-call | tf_op jit(solution)/shard_map/pallas_call | solution.py:554
  70.3 1.4 %shard_map.103 = (bf16[1,128,3072]{2,1,0:T(8,128)(2,1)}, bf16[1,128,3072]{2,1,0:T(8,128)(2,1)}, bf16[1,128,3072]{2,1,0:T(8,128)(2,1)}, f32[2,128]{1,0:T(2,128)}) custom-call(bf16[1,128,3072]{2,1,0:T(8,128)(2,1)S(1)} %get-tuple-element.8.refs_0_, bf16[1,128,3072]{2,1,0:T(8,128)(2,1)S(1)} %get-tuple-element.9.refs_1_, ...), custom_call_target="tpu_custom_call" | custom-call | tf_op jit(solution)/shard_map/pallas_call | solution.py:596
where the time goes:
time: 71.9 us; the launch traced here: 71.7 us
  Pallas kernels  71.1 us (99%)
    pallas_call x1, Pallas kernels, exchange_body(): pl.pallas_call(functools.partial(exchange_kernel, units, groups, gain_sca...  69.6 us

commit v1 on v0

--- a/solution.py
+++ b/solution.py
@@ -253,13 +253,21 @@
 
 def head_work(slot, arrived, results, gain_acc, gains, scratch):
     bias, q_norm, k_norm, k_cols, grad_qn, grad_kn, grad_v, scores, grads, probs_half, grads_half = scratch
-    seq_len = arrived.shape[2]
+    _, units, _, tok_rows, _ = arrived.shape
+    seq_len = units * tok_rows
     block_count = seq_len // BLOCK
+    tile_units = QUERY_TILE // tok_rows
     score_scale = HEAD_DIM ** (-0.5)
     exponent_scale = score_scale * math.log2(math.e)
 
+    def rows_for(which):
+        return arrived[slot, :, which].reshape(seq_len, HEAD_DIM)
+
+    def put(which, grad):
+        results[slot, :, which] = grad.astype(jnp.bfloat16).reshape(units, tok_rows, HEAD_DIM)
+
     def normed(which):
-        raw = arrived[slot, which].astype(jnp.float32)
+        raw = rows_for(which).astype(jnp.float32)
         inverse = 1.0 / jnp.sqrt(jnp.mean(raw * raw, axis=1, keepdims=True) + norm_eps)
         return raw * inverse * gains[which][...]
 
@@ -273,7 +281,7 @@
     def tile_step(tile, carry):
         rows = aligned(tile, QUERY_TILE)
         q_tile = q_norm[rows, :]
-        o_tile = arrived[slot, 3, rows, :]
+        o_tile = arrived[slot, pl.ds(tile * tile_units, tile_units), 3].reshape(QUERY_TILE, HEAD_DIM)
         shifts = bias[:, rows]
         peak = jnp.full((1, QUERY_TILE), -jnp.inf, jnp.float32)
         for block in range(block_count):
@@ -288,7 +296,7 @@
             keys = pl.ds(block * BLOCK, BLOCK)
             offset = shifts[block : block + 1, :] - peak
             weights = jnp.exp2(scores[keys, :] * exponent_scale + offset)
-            grad_weights = dot_rows(arrived[slot, 2, keys, :], o_tile)
+            grad_weights = dot_rows(arrived[slot, block, 2], o_tile)
             scores[keys, :] = weights
             grads[keys, :] = grad_weights
             total = total + jnp.sum(weights, axis=0, keepdims=True)
@@ -307,118 +315,103 @@
         return carry
 
     lax.fori_loop(0, seq_len // QUERY_TILE, tile_step, 0)
-    results[slot, 2] = grad_v[...].astype(jnp.bfloat16)
+    put(2, grad_v[...])
     for which, grad_normed in ((0, grad_qn), (1, grad_kn)):
-        raw = arrived[slot, which].astype(jnp.float32)
+        raw = rows_for(which).astype(jnp.float32)
         inverse = 1.0 / jnp.sqrt(jnp.mean(raw * raw, axis=1, keepdims=True) + norm_eps)
         unit = raw * inverse
         grad = grad_normed[...] * score_scale
         gain_acc[which : which + 1, :] += jnp.sum(grad * unit, axis=0, keepdims=True)
         scaled = grad * gains[which][...]
         inner = jnp.mean(scaled * unit, axis=1, keepdims=True)
-        results[slot, which] = ((scaled - unit * inner) * inverse).astype(jnp.bfloat16)
+        put(which, (scaled - unit * inner) * inverse)
 
 
 def exchange_kernel(
     units, groups, gain_scale,
     q_raw, k_raw, values, grad_out, q_gain_in, k_gain_in, masks_in,
-    out_q, out_k, out_v, out_gain,
-    arrived, results, gain_units, gain_groups, gain_acc,
-    in_send, in_recv, in_own, out_send, out_recv, out_own,
+    landed, out_gain,
+    staged, arrived, results, gain_units, gain_groups, gain_acc,
+    stage_sem, in_send, in_recv, in_own, out_send, out_recv, out_own,
     unit_send, unit_recv, group_send, group_recv, small_sem, q_gain, k_gain, masks, *scratch,
 ):
     me = lax.axis_index("ulysses")
     group = lax.axis_index("dp")
-    slots, _, seq_len, _ = arrived.shape
-    tok_rows = seq_len // units
+    slots = arrived.shape[0]
     sources = (q_raw, k_raw, values, grad_out)
-    targets = (out_q, out_k, out_v)
-
     bits = units.bit_length() - 1
-    paired = units == 2**bits
+    group_bits = groups.bit_length() - 1
+
+    def flipped(index, offset, count):
+        places = (lax.rem(index // 2**bit + offset // 2**bit, 2) * 2**bit for bit in range(count))
+        return sum(places, jnp.int32(0))
 
     def unit_at(offset):
-        if not paired:
-            return lax.rem(me + offset % units, units)
-        places = (lax.rem(me // 2**bit + offset // 2**bit, 2) * 2**bit for bit in range(bits))
-        return sum(places, jnp.int32(0))
-
-    def sender_at(offset):
-        return unit_at(offset if paired else units - offset)
+        return flipped(me, offset, bits)
 
     offsets = sorted(range(1, units), key=lambda offset: (-(offset // 2).bit_count(), offset % 2, offset))
 
-    def group_at(offset):
-        return lax.rem(group + offset, groups)
-
-    def inward(slot, which, offset):
+    def stage(slot, owner, which):
+        return pltpu.make_async_copy(
+            sources[which].at[0, :, aligned(owner * slots + slot, HEAD_DIM)],
+            staged.at[slot, owner, which],
+            stage_sem.at[slot],
+        )
+
+    def remote(source, target, send_sem, recv_sem, device):
+        return pltpu.make_async_remote_copy(
+            src_ref=source,
+            dst_ref=target,
+            send_sem=send_sem,
+            recv_sem=recv_sem,
+            device_id=device,
+            device_id_type=MESH,
+        )
+
+    def inward(slot, offset):
         owner = unit_at(offset)
-        return pltpu.make_async_remote_copy(
-            src_ref=sources[which].at[0, :, aligned(owner * slots + slot, HEAD_DIM)],
-            dst_ref=arrived.at[slot, which, aligned(me, tok_rows), :],
-            send_sem=in_send.at[slot, which, offset],
-            recv_sem=in_recv.at[slot, which, offset],
-            device_id={"ulysses": owner},
-            device_id_type=MESH,
+        return remote(
+            staged.at[slot, owner], arrived.at[slot, me],
+            in_send.at[slot, offset], in_recv.at[slot, offset], {"ulysses": owner},
         )
 
     def inward_own(slot, which):
         return pltpu.make_async_copy(
             sources[which].at[0, :, aligned(me * slots + slot, HEAD_DIM)],
-            arrived.at[slot, which, aligned(me, tok_rows), :],
+            arrived.at[slot, me, which],
             in_own.at[slot, which],
         )
 
-    def inward_from(slot, which, offset):
-        owner = sender_at(offset)
-        landed = arrived.at[slot, which, aligned(owner, tok_rows), :]
-        return pltpu.make_async_remote_copy(
-            src_ref=landed,
-            dst_ref=landed,
-            send_sem=in_send.at[slot, which, offset],
-            recv_sem=in_recv.at[slot, which, offset],
-            device_id={"ulysses": owner},
-            device_id_type=MESH,
-        )
-
-    def outward(slot, which, offset):
+    def inward_from(slot, offset):
         owner = unit_at(offset)
-        return pltpu.make_async_remote_copy(
-            src_ref=results.at[slot, which, aligned(owner, tok_rows), :],
-            dst_ref=targets[which].at[0, :, aligned(me * slots + slot, HEAD_DIM)],
-            send_sem=out_send.at[slot, which, offset],
-            recv_sem=out_recv.at[slot, which, offset],
-            device_id={"ulysses": owner},
-            device_id_type=MESH,
-        )
-
-    def outward_own(slot, which):
+        place = arrived.at[slot, owner]
+        return remote(place, place, in_send.at[slot, offset], in_recv.at[slot, offset], {"ulysses": owner})
+
+    def outward(slot, offset):
+        owner = unit_at(offset)
+        return remote(
+            results.at[slot, owner], landed.at[me * slots + slot],
+            out_send.at[slot, offset], out_recv.at[slot, offset], {"ulysses": owner},
+        )
+
+    def outward_own(slot):
         return pltpu.make_async_copy(
-            results.at[slot, which, aligned(me, tok_rows), :],
-            targets[which].at[0, :, aligned(me * slots + slot, HEAD_DIM)],
-            out_own.at[slot, which],
-        )
-
-    def outward_from(slot, which, offset):
-        owner = sender_at(offset)
-        landed = targets[which].at[0, :, aligned(owner * slots + slot, HEAD_DIM)]
-        return pltpu.make_async_remote_copy(
-            src_ref=landed,
-            dst_ref=landed,
-            send_sem=out_send.at[slot, which, offset],
-            recv_sem=out_recv.at[slot, which, offset],
-            device_id={"ulysses": owner},
-            device_id_type=MESH,
-        )
-
-    def gain_to(buffer, place, axis, target, send_sem, recv_sem):
-        return pltpu.make_async_remote_copy(
-            src_ref=buffer.at[place],
-            dst_ref=buffer.at[place],
-            send_sem=send_sem,
-            recv_sem=recv_sem,
-            device_id={axis: target},
-            device_id_type=MESH,
+            results.at[slot, me], landed.at[me * slots + slot], out_own.at[slot]
+        )
+
+    def outward_from(slot, offset):
+        owner = unit_at(offset)
+        place = landed.at[owner * slots + slot]
+        return remote(place, place, out_send.at[slot, offset], out_recv.at[slot, offset], {"ulysses": owner})
+
+    def unit_gain(place, offset):
+        block = gain_units.at[place]
+        return remote(block, block, unit_send.at[offset], unit_recv.at[offset], {"ulysses": unit_at(offset)})
+
+    def group_gain(bit):
+        return remote(
+            gain_groups.at[bit, 0], gain_groups.at[bit, 1],
+            group_send.at[bit], group_recv.at[bit], {"dp": flipped(group, 2**bit, group_bits)},
         )
 
     small_copies = [
@@ -430,23 +423,33 @@
     barrier = pltpu.get_barrier_semaphore()
     for offset in offsets:
         pl.semaphore_signal(barrier, inc=1, device_id={"ulysses": unit_at(offset)}, device_id_type=MESH)
-    for offset in range(1, groups):
-        pl.semaphore_signal(barrier, inc=1, device_id={"dp": group_at(offset)}, device_id_type=MESH)
+    for bit in range(group_bits):
+        pl.semaphore_signal(
+            barrier, inc=1, device_id={"dp": flipped(group, 2**bit, group_bits)}, device_id_type=MESH
+        )
+
+    def fetch_slot(slot, carry):
+        for owner in range(units):
+            for which in range(4):
+                stage(slot, owner, which).start()
+        return carry
+
+    lax.fori_loop(0, slots, fetch_slot, 0)
     for copy in small_copies:
         copy.start()
     for slot in range(slots):
         for which in range(4):
             inward_own(slot, which).start()
-    pl.semaphore_wait(barrier, units + groups - 2)
+    gain_acc[...] = jnp.zeros_like(gain_acc)
+    pl.semaphore_wait(barrier, units - 1 + group_bits)
 
     def send_slot(slot, carry):
+        pltpu.make_async_copy(staged.at[slot], staged.at[slot], stage_sem.at[slot]).wait()
         for offset in offsets:
-            for which in range(4):
-                inward(slot, which, offset).start()
+            inward(slot, offset).start()
         return carry
 
     lax.fori_loop(0, slots, send_slot, 0)
-    gain_acc[...] = jnp.zeros_like(gain_acc)
     for copy in small_copies:
         copy.wait()
     bias = scratch[0]
@@ -461,75 +464,62 @@
             bias[:, block * BLOCK : (block + 1) * BLOCK] = jnp.broadcast_to(shift, (block_count, BLOCK))
         for which in range(4):
             inward_own(slot, which).wait()
-            for offset in offsets:
-                inward_from(slot, which, offset).wait_recv()
+        for offset in offsets:
+            inward_from(slot, offset).wait_recv()
         head_work(slot, arrived, results, gain_acc, (q_gain, k_gain), scratch)
 
         @pl.when(slot == slots - 1)
         def _():
             gain_units[me] = gain_acc[...]
             for offset in offsets:
-                gain_to(
-                    gain_units, me, "ulysses", unit_at(offset), unit_send.at[offset], unit_recv.at[offset]
-                ).start()
+                unit_gain(me, offset).start()
 
         for offset in offsets:
-            for which in range(3):
-                outward(slot, which, offset).start()
-        for which in range(3):
-            outward_own(slot, which).start()
+            outward(slot, offset).start()
+        outward_own(slot).start()
         return carry
 
     lax.fori_loop(0, slots, work_slot, 0)
 
     for offset in offsets:
-        sender = sender_at(offset)
-        gain_to(
-            gain_units, sender, "ulysses", sender, unit_send.at[offset], unit_recv.at[offset]
-        ).wait_recv()
-    gain_groups[group] = jnp.sum(gain_units[...], axis=0)
-    for offset in range(1, groups):
-        gain_to(
-            gain_groups, group, "dp", group_at(offset), group_send.at[offset], group_recv.at[offset]
-        ).start()
-    for offset in range(1, groups):
-        sender = group_at(groups - offset)
-        gain_to(
-            gain_groups, sender, "dp", sender, group_send.at[offset], group_recv.at[offset]
-        ).wait_recv()
-    out_gain[...] = jnp.sum(gain_groups[...], axis=0)[:2] * gain_scale
+        unit_gain(unit_at(offset), offset).wait_recv()
+    gain_sum = jnp.sum(gain_units[...], axis=0)
+    for bit in range(group_bits):
+        gain_groups[bit, 0] = gain_sum
+        group_gain(bit).start()
+        group_gain(bit).wait_recv()
+        gain_sum = gain_sum + gain_groups[bit, 1]
+    out_gain[...] = gain_sum[:2] * gain_scale
 
     def drain_slot(slot, carry):
         for offset in offsets:
-            for which in range(4):
-                inward(slot, which, offset).wait_send()
-            for which in range(3):
-                outward(slot, which, offset).wait_send()
-                outward_from(slot, which, offset).wait_recv()
-        for which in range(3):
-            outward_own(slot, which).wait()
+            inward(slot, offset).wait_send()
+            outward(slot, offset).wait_send()
+            outward_from(slot, offset).wait_recv()
+        outward_own(slot).wait()
         return carry
 
     lax.fori_loop(0, slots, drain_slot, 0)
     for offset in offsets:
-        gain_to(
-            gain_units, me, "ulysses", unit_at(offset), unit_send.at[offset], unit_recv.at[offset]
-        ).wait_send()
-    for offset in range(1, groups):
-        gain_to(
-            gain_groups, group, "dp", group_at(offset), group_send.at[offset], group_recv.at[offset]
-        ).wait_send()
-
-
-def hand_on_kernel(*refs):
-    *arrays, sems = refs
-    copies = [
-        pltpu.make_async_copy(arrays[place], arrays[place + 4], sems.at[place]) for place in range(4)
-    ]
-    for copy in copies:
-        copy.start()
-    for copy in copies:
-        copy.wait()
+        unit_gain(me, offset).wait_send()
+    for bit in range(group_bits):
+        group_gain(bit).wait_send()
+
+
+def hand_on_kernel(landed, gain_in, out_q, out_k, out_v, out_gain, sems, gain_sem):
+    targets = (out_q, out_k, out_v)
+    gain_copy = pltpu.make_async_copy(gain_in, out_gain, gain_sem)
+    gain_copy.start()
+    for head in range(landed.shape[0]):
+        for which in range(3):
+            pltpu.make_async_copy(
+                landed.at[head, which],
+                targets[which].at[0, :, pl.ds(head * HEAD_DIM, HEAD_DIM)],
+                sems.at[which],
+            ).start()
+    for which in range(3):
+        pltpu.make_async_copy(targets[which], targets[which], sems.at[which]).wait()
+    gain_copy.wait()
 
 
 def exchange_body(q_raw, k_raw, values, grad_out, q_gain, k_gain, block_masks):
@@ -538,6 +528,7 @@
     _, tok_rows, width = q_raw.shape
     seq_len = tok_rows * units
     slots = HEADS // units
+    group_bits = groups.bit_length() - 1
     block_count = block_masks.shape[1]
     gain_scale = (groups * seq_len * HEADS) ** (-0.5)
     in_vmem = pl.BlockSpec(memory_space=pltpu.VMEM)
@@ -546,32 +537,35 @@
     shard = jax.ShapeDtypeStruct((1, tok_rows, width), jnp.bfloat16)
     half = jnp.bfloat16
     full = jnp.float32
+    small = jax.ShapeDtypeStruct((2, HEAD_DIM), full)
     dma = pltpu.SemaphoreType.DMA
     operands = (
         q_raw, k_raw, values, grad_out,
         q_gain.reshape(1, HEAD_DIM), k_gain.reshape(1, HEAD_DIM), block_masks.transpose(1, 2, 0),
     )
-    grad_q, grad_k, grad_v, gain_grads = pl.pallas_call(
+    landed, gain_grads = pl.pallas_call(
         functools.partial(exchange_kernel, units, groups, gain_scale),
-        out_shape=(shard, shard, shard, jax.ShapeDtypeStruct((2, HEAD_DIM), full)),
+        out_shape=(jax.ShapeDtypeStruct((HEADS, 3, tok_rows, HEAD_DIM), half), small),
         in_specs=[in_hbm] * 7,
-        out_specs=(anywhere, anywhere, anywhere, in_vmem),
+        out_specs=(anywhere, in_vmem),
         scratch_shapes=[
-            pltpu.VMEM((slots, 4, seq_len, HEAD_DIM), half),
-            pltpu.VMEM((slots, 3, seq_len, HEAD_DIM), half),
+            pltpu.VMEM((slots, units, 4, tok_rows, HEAD_DIM), half),
+            pltpu.VMEM((slots, units, 4, tok_rows, HEAD_DIM), half),
+            pltpu.VMEM((slots, units, 3, tok_rows, HEAD_DIM), half),
             pltpu.VMEM((units, 8, HEAD_DIM), full),
-            pltpu.VMEM((groups, 8, HEAD_DIM), full),
+            pltpu.VMEM((max(1, group_bits), 2, 8, HEAD_DIM), full),
             pltpu.VMEM((8, HEAD_DIM), full),
-            dma((slots, 4, units)),
-            dma((slots, 4, units)),
+            dma((slots,)),
+            dma((slots, units)),
+            dma((slots, units)),
             dma((slots, 4)),
-            dma((slots, 3, units)),
-            dma((slots, 3, units)),
-            dma((slots, 3)),
+            dma((slots, units)),
+            dma((slots, units)),
+            dma((slots,)),
             dma((units,)),
             dma((units,)),
-            dma((groups,)),
-            dma((groups,)),
+            dma((max(1, group_bits),)),
+            dma((max(1, group_bits),)),
             dma((3,)),
             pltpu.VMEM((1, HEAD_DIM), full),
             pltpu.VMEM((1, HEAD_DIM), full),
@@ -592,22 +586,22 @@
     )(
         *(pltpu.with_memory_space_constraint(operand, pltpu.HBM) for operand in operands)
     )
-    small = jax.ShapeDtypeStruct((2, HEAD_DIM), full)
     return pl.pallas_call(
         hand_on_kernel,
         out_shape=(shard, shard, shard, small),
-        in_specs=[anywhere] * 4,
+        in_specs=[anywhere] * 2,
         out_specs=[in_hbm] * 4,
-        scratch_shapes=[dma((4,))],
+        scratch_shapes=[dma((3,)), dma(())],
         compiler_params=pltpu.CompilerParams(vmem_limit_bytes=2**20),
-    )(grad_q, grad_k, grad_v, gain_grads)
+    )(landed, gain_grads)
 
 
 def solution(mesh):
     units = mesh.shape["ulysses"]
+    even = all(size == 2 ** (size.bit_length() - 1) for size in (units, mesh.shape["dp"]))
 
     def chosen(q_raw, *rest):
-        if HEADS % units == 0 and q_raw.shape[0] == 1:
+        if even and HEADS % units == 0 and q_raw.shape[:2] == (1, BLOCK):
             return exchange_body(q_raw, *rest)
         return body(q_raw, *rest)
 

time: 71.9 us -> 68.6 us (0.954)
  Pallas kernels: 71.1 us -> 67.6 us
    pallas_call x1, Pallas kernels: 69.6 us -> 66.2 us  [exchange_body(): pl.pallas_call(functools.partial(exchange_kernel, units, groups, gain_sca...]
where the time goes in v1:
time: 68.6 us; the launch traced here: 68.2 us
  Pallas kernels  67.6 us (99%)
    pallas_call x1, Pallas kernels, exchange_body(): pl.pallas_call(functools.partial(exchange_kernel, units, groups, gain_sca...  66.2 us
    pallas_call x1, Pallas kernels, exchange_body(): pl.pallas_call(hand_on_kernel, out_shape=(shard, shard, shard, small), in...  1.41 us

profile of v1, /device:TPU:1, one launch (start us, length us, event | category | flops | bytes accessed | tf_op | source)
XLA Modules:
  0.0 68.2 jit_solution(13694335588742763796)
XLA Ops:
  0.6 66.2 %shard_map.102 = (bf16[24,3,128,128]{3,2,1,0:T(8,128)(2,1)S(1)}, f32[2,128]{1,0:T(2,128)S(1)}) custom-call(bf16[1,128,3072]{2,1,0:T(8,128)(2,1)} %q_raw.1, bf16[1,128,3072]{2,1,0:T(8,128)(2,1)} %k_raw.1, bf16[1,128,3072]{2,1,0:T(8,128)(2,1)} %values.1, bf16[1,128,3072]{2,1,0:T(8,128)(2,1)} %grad_out.1, f32[1,128]{1,0:T(1,128)} %bitcast.4, f32[1,128]{1,0:T(1,128)} %bitcast.5, ...), custom_call_target="tpu_custom_call" | custom-call | tf_op jit(solution)/shard_map/pallas_call | solution.py:546
  66.8 1.4 %shard_map.103 = (bf16[1,128,3072]{2,1,0:T(8,128)(2,1)}, bf16[1,128,3072]{2,1,0:T(8,128)(2,1)}, bf16[1,128,3072]{2,1,0:T(8,128)(2,1)}, f32[2,128]{1,0:T(2,128)}) custom-call(bf16[24,3,128,128]{3,2,1,0:T(8,128)(2,1)S(1)} %get-tuple-element.6.landed, f32[2,128]{1,0:T(2,128)S(1)} %get-tuple-element.7.gain_in), custom_call_target="tpu_custom_call" | custom-call | tf_op jit(solution)/shard_map/pallas_call | solution.py:589

commit v2 on v1

--- a/solution.py
+++ b/solution.py
@@ -470,7 +470,13 @@
 
         @pl.when(slot == slots - 1)
         def _():
-            gain_units[me] = gain_acc[...]
+            gain_sum = gain_acc[...]
+            for bit in range(group_bits):
+                gain_groups[bit, 0] = gain_sum
+                group_gain(bit).start()
+                group_gain(bit).wait_recv()
+                gain_sum = gain_sum + gain_groups[bit, 1]
+            gain_units[me] = gain_sum
             for offset in offsets:
                 unit_gain(me, offset).start()
 
@@ -483,13 +489,7 @@
 
     for offset in offsets:
         unit_gain(unit_at(offset), offset).wait_recv()
-    gain_sum = jnp.sum(gain_units[...], axis=0)
-    for bit in range(group_bits):
-        gain_groups[bit, 0] = gain_sum
-        group_gain(bit).start()
-        group_gain(bit).wait_recv()
-        gain_sum = gain_sum + gain_groups[bit, 1]
-    out_gain[...] = gain_sum[:2] * gain_scale
+    out_gain[...] = jnp.sum(gain_units[...], axis=0)[:2] * gain_scale
 
     def drain_slot(slot, carry):
         for offset in offsets:

time: 68.6 us -> 68.4 us (level)
  no operation moved by 1% of the time
where the time goes in v2:
time: 68.4 us; the launch traced here: 68.2 us
  Pallas kernels  67.6 us (99%)
    pallas_call x1, Pallas kernels, exchange_body(): pl.pallas_call(functools.partial(exchange_kernel, units, groups, gain_sca...  66.2 us
    pallas_call x1, Pallas kernels, exchange_body(): pl.pallas_call(hand_on_kernel, out_shape=(shard, shard, shard, small), in...  1.41 us

profile of v2, /device:TPU:1, one launch (start us, length us, event | category | flops | bytes accessed | tf_op | source)
XLA Modules:
  0.0 68.2 jit_solution(16094581781595529987)
XLA Ops:
  0.6 66.2 %shard_map.102 = (bf16[24,3,128,128]{3,2,1,0:T(8,128)(2,1)S(1)}, f32[2,128]{1,0:T(2,128)S(1)}) custom-call(bf16[1,128,3072]{2,1,0:T(8,128)(2,1)} %q_raw.1, bf16[1,128,3072]{2,1,0:T(8,128)(2,1)} %k_raw.1, bf16[1,128,3072]{2,1,0:T(8,128)(2,1)} %values.1, bf16[1,128,3072]{2,1,0:T(8,128)(2,1)} %grad_out.1, f32[1,128]{1,0:T(1,128)} %bitcast.4, f32[1,128]{1,0:T(1,128)} %bitcast.5, ...), custom_call_target="tpu_custom_call" | custom-call | tf_op jit(solution)/shard_map/pallas_call | solution.py:546
  66.8 1.4 %shard_map.103 = (bf16[1,128,3072]{2,1,0:T(8,128)(2,1)}, bf16[1,128,3072]{2,1,0:T(8,128)(2,1)}, bf16[1,128,3072]{2,1,0:T(8,128)(2,1)}, f32[2,128]{1,0:T(2,128)}) custom-call(bf16[24,3,128,128]{3,2,1,0:T(8,128)(2,1)S(1)} %get-tuple-element.6.landed, f32[2,128]{1,0:T(2,128)S(1)} %get-tuple-element.7.gain_in), custom_call_target="tpu_custom_call" | custom-call | tf_op jit(solution)/shard_map/pallas_call | solution.py:589

commit v3 on v2

--- a/solution.py
+++ b/solution.py
@@ -355,7 +355,7 @@
         return pltpu.make_async_copy(
             sources[which].at[0, :, aligned(owner * slots + slot, HEAD_DIM)],
             staged.at[slot, owner, which],
-            stage_sem.at[slot],
+            stage_sem.at[slot, owner],
         )
 
     def remote(source, target, send_sem, recv_sem, device):
@@ -429,9 +429,9 @@
         )
 
     def fetch_slot(slot, carry):
-        for owner in range(units):
+        for offset in offsets:
             for which in range(4):
-                stage(slot, owner, which).start()
+                stage(slot, unit_at(offset), which).start()
         return carry
 
     lax.fori_loop(0, slots, fetch_slot, 0)
@@ -444,8 +444,9 @@
     pl.semaphore_wait(barrier, units - 1 + group_bits)
 
     def send_slot(slot, carry):
-        pltpu.make_async_copy(staged.at[slot], staged.at[slot], stage_sem.at[slot]).wait()
         for offset in offsets:
+            block = staged.at[slot, unit_at(offset)]
+            pltpu.make_async_copy(block, block, stage_sem.at[slot, unit_at(offset)]).wait()
             inward(slot, offset).start()
         return carry
 
@@ -555,7 +556,7 @@
             pltpu.VMEM((units, 8, HEAD_DIM), full),
             pltpu.VMEM((max(1, group_bits), 2, 8, HEAD_DIM), full),
             pltpu.VMEM((8, HEAD_DIM), full),
-            dma((slots,)),
+            dma((slots, units)),
             dma((slots, units)),
             dma((slots, units)),
             dma((slots, 4)),

time: 68.4 us -> 68.6 us (level)
  no operation moved by 1% of the time
where the time goes in v3:
time: 68.6 us; the launch traced here: 68.4 us
  Pallas kernels  67.8 us (99%)
    pallas_call x1, Pallas kernels, exchange_body(): pl.pallas_call(functools.partial(exchange_kernel, units, groups, gain_sca...  66.4 us
    pallas_call x1, Pallas kernels, exchange_body(): pl.pallas_call(hand_on_kernel, out_shape=(shard, shard, shard, small), in...  1.41 us

profile of v3, /device:TPU:1, one launch (start us, length us, event | category | flops | bytes accessed | tf_op | source)
XLA Modules:
  0.0 68.4 jit_solution(11274608030682631384)
XLA Ops:
  0.6 66.4 %shard_map.102 = (bf16[24,3,128,128]{3,2,1,0:T(8,128)(2,1)S(1)}, f32[2,128]{1,0:T(2,128)S(1)}) custom-call(bf16[1,128,3072]{2,1,0:T(8,128)(2,1)} %q_raw.1, bf16[1,128,3072]{2,1,0:T(8,128)(2,1)} %k_raw.1, bf16[1,128,3072]{2,1,0:T(8,128)(2,1)} %values.1, bf16[1,128,3072]{2,1,0:T(8,128)(2,1)} %grad_out.1, f32[1,128]{1,0:T(1,128)} %bitcast.4, f32[1,128]{1,0:T(1,128)} %bitcast.5, ...), custom_call_target="tpu_custom_call" | custom-call | tf_op jit(solution)/shard_map/pallas_call | solution.py:547
  67.0 1.4 %shard_map.103 = (bf16[1,128,3072]{2,1,0:T(8,128)(2,1)}, bf16[1,128,3072]{2,1,0:T(8,128)(2,1)}, bf16[1,128,3072]{2,1,0:T(8,128)(2,1)}, f32[2,128]{1,0:T(2,128)}) custom-call(bf16[24,3,128,128]{3,2,1,0:T(8,128)(2,1)S(1)} %get-tuple-element.6.landed, f32[2,128]{1,0:T(2,128)S(1)} %get-tuple-element.7.gain_in), custom_call_target="tpu_custom_call" | custom-call | tf_op jit(solution)/shard_map/pallas_call | solution.py:590
